TPU v7x, 256 devices: a whole 4x4x8 slice. The times are simulated.
256 devices in a mesh: dp: 32 (over z, y_hi, core), mp: 8 (over x, y_lo).
Axes of the slice: x: 4, y: 4 (y_hi: 2, y_lo: 2; y = y_hi * 2 + y_lo), z: 8, core: 2. Of those that a mesh axis runs over, the one named last changes fastest.
Arguments:
- token_ids: int32 [128, 64], P(None, 'dp'), may hold values from 0 to 1023
- fanout: int32 [128, 16], replicated, may hold values from 1 to 16
- table_of_column: int32 [64], P('dp'), may hold values from 0 to 15
- embed_table: bfloat16 [64, 1024, 1024], P('dp', 'mp'), may hold values from -35 to 35
- start_vector: bfloat16 [1024], replicated, may hold values from -6 to 6
- gain_attn: bfloat16 [1024], replicated, may hold values from 0.25 to 1.75
- gain_mlp: bfloat16 [1024], replicated, may hold values from 0.25 to 1.75
- gain_final: bfloat16 [1024], replicated, may hold values from 0.25 to 1.75
- w_qkv: bfloat16 [1024, 3, 1024], P(None, None, 'mp'), may hold values from -8 to 8
- w_out: bfloat16 [1024, 1024], P(None, 'mp'), may hold values from -0.1875 to 0.1875
- w_gate: bfloat16 [1024, 4096], P(None, 'mp'), may hold values from -0.1875 to 0.1875
- w_up: bfloat16 [1024, 4096], P(None, 'mp'), may hold values from -0.1875 to 0.1875
- w_down: bfloat16 [1024, 4096], P(None, 'mp'), may hold values from -0.09375 to 0.09375
Outputs:
- nll: float32 [128, 64], P(None, 'dp')
- grad_table: float32 [64, 1024, 1024], P('dp', 'mp')
- grad_qkv: float32 [1024, 3, 1024], P('dp', None, 'mp')
- grad_out: float32 [1024, 1024], P('dp', 'mp')
- grad_gate: float32 [1024, 4096], P('dp', 'mp')
- grad_up: float32 [1024, 4096], P('dp', 'mp')
- grad_down: float32 [1024, 4096], P('dp', 'mp')
All inputs are finite; a program needn't handle non-finite values.
Results may differ from a plain program's by a relative error of at most 0.015.
The roundings to bfloat16 on the way count: a program that leaves them out, or rounds other values in their place, can miss the bound.
Values may be sent and summed in bfloat16 or wider, within the bound.
A program may use at most 128 MiB of HBM per device.

v0:
```python
import math
import jax
import jax.numpy as jnp
from jax import lax
from jax.sharding import PartitionSpec as P

HS = 64
TABLES = 16
EPS = 1e-05
ATTN_CAP = 50.0
LOGIT_CAP = 30.0


def gather_features(values):
    return lax.all_gather(values, "mp", axis=2, tiled=True)


def feature_sum(term):
    return lax.psum_scatter(term, "mp", scatter_dimension=2, tiled=True)


def cols_to_rows(values):
    return lax.all_to_all(values, "dp", split_axis=0, concat_axis=1, tiled=True)


def rows_to_cols(values):
    return lax.all_to_all(values, "dp", split_axis=1, concat_axis=0, tiled=True)


def rms_of(values):
    floats = values.astype(jnp.float32)
    return jnp.sqrt(jnp.mean(floats * floats, axis=-1, keepdims=True) + EPS)


def normalize(values, gain, rms):
    return (values.astype(jnp.float32) / rms * gain.astype(jnp.float32)).astype(jnp.bfloat16)


def norm_back_full(values, d_norm, gain, rms):
    floats = values.astype(jnp.float32)
    gains = gain.astype(jnp.float32)
    total = jnp.sum(gains * d_norm * floats, axis=-1, keepdims=True)
    return gains * d_norm / rms - floats * total / (floats.shape[-1] * rms * rms * rms)


def norm_back_part(values, d_norm, gain, rms, model_width):
    floats = values.astype(jnp.float32)
    gains = gain.astype(jnp.float32)
    partial_total = jnp.sum(gains * d_norm * floats, axis=-1)
    total = lax.psum(partial_total, "mp")[..., None]
    return gains * d_norm / rms - floats * total / (model_width * rms * rms * rms)


def local(
    token_ids,
    fanout,
    table_of_column,
    embed_table,
    start_vector,
    gain_attn,
    gain_mlp,
    gain_final,
    w_qkv,
    w_out,
    w_gate,
    w_up,
    w_down,
):
    fl = jnp.float32
    mp_rank = lax.axis_index("mp")
    mp_count = lax.axis_size("mp")
    model_width = embed_table.shape[2]
    vocab_part = embed_table.shape[1]
    part_width = model_width // mp_count
    head_cols = w_qkv.shape[2]
    local_heads = head_cols // HS
    row_total_count = token_ids.shape[0]

    def own_part(vector):
        return lax.dynamic_slice_in_dim(vector, mp_rank * part_width, part_width, 0)

    local_ids = token_ids - mp_rank * vocab_part
    onehot = (
        local_ids[:, :, None] == jnp.arange(vocab_part, dtype=jnp.int32)[None, None, :]
    ).astype(jnp.bfloat16)
    picked = jnp.einsum("rcv,cvd->rcd", onehot, embed_table, preferred_element_type=fl)
    emb_cols = feature_sum(picked).astype(jnp.bfloat16)
    emb_rows = cols_to_rows(emb_cols)
    rows_here = emb_rows.shape[0]
    col_count = emb_rows.shape[1]
    start_rows = jnp.broadcast_to(own_part(start_vector)[None, None, :], (rows_here, 1, part_width))
    resid_in = jnp.concatenate([start_rows, emb_rows[:, :-1]], axis=1)
    in_full = gather_features(resid_in)
    rms_attn = rms_of(in_full)
    norm_attn = normalize(in_full, gain_attn, rms_attn)
    qkv = jnp.einsum("rpd,dtx->rptx", norm_attn, w_qkv, preferred_element_type=fl).astype(
        jnp.bfloat16
    )
    queries = qkv[:, :, 0].reshape(rows_here, col_count, local_heads, HS)
    key_rows = qkv[:, :, 1].reshape(rows_here, col_count, local_heads, HS)
    value_rows = qkv[:, :, 2].reshape(rows_here, col_count, local_heads, HS)
    score_raw = jnp.einsum(
        "rqhe,rkhe->rhqk", queries, key_rows, preferred_element_type=fl
    ) / math.sqrt(HS)
    score = ATTN_CAP * jnp.tanh(score_raw / ATTN_CAP)
    col_index = jnp.arange(col_count, dtype=jnp.int32)
    causal = col_index[:, None] >= col_index[None, :]
    exp_score = jnp.where(causal, jnp.exp(score), 0.0)
    attn_prob = exp_score / jnp.sum(exp_score, axis=-1, keepdims=True)
    prob_b = attn_prob.astype(jnp.bfloat16)
    attn_heads = jnp.einsum(
        "rhqk,rkhe->rqhe", prob_b, value_rows, preferred_element_type=fl
    ).astype(jnp.bfloat16)
    attn_out = attn_heads.reshape(rows_here, col_count, head_cols)
    mixed_part = jnp.einsum("rpj,dj->rpd", attn_out, w_out, preferred_element_type=fl)
    resid_mid = (resid_in.astype(fl) + feature_sum(mixed_part)).astype(jnp.bfloat16)
    mid_full = gather_features(resid_mid)
    rms_mlp = rms_of(mid_full)
    norm_mlp = normalize(mid_full, gain_mlp, rms_mlp)
    gate_pre = jnp.einsum("rpd,df->rpf", norm_mlp, w_gate, preferred_element_type=fl)
    up_proj = jnp.einsum("rpd,df->rpf", norm_mlp, w_up, preferred_element_type=fl)
    hidden = (jax.nn.silu(gate_pre) * up_proj).astype(jnp.bfloat16)
    down_part = jnp.einsum("rpf,df->rpd", hidden, w_down, preferred_element_type=fl)
    resid_out = (resid_mid.astype(fl) + feature_sum(down_part)).astype(jnp.bfloat16)
    out_cols = rows_to_cols(resid_out)
    out_full = gather_features(out_cols)
    rms_final = rms_of(out_full)
    norm_final = normalize(out_full, gain_final, rms_final)
    width_root = math.sqrt(model_width)
    logit_raw = (
        jnp.einsum("rcd,cvd->rcv", norm_final, embed_table, preferred_element_type=fl) / width_root
    )
    capped = LOGIT_CAP * jnp.tanh(logit_raw / LOGIT_CAP)
    exp_logit = jnp.exp(capped)
    onehot_f = onehot.astype(fl)
    exp_total, target_logit = lax.psum(
        (jnp.sum(exp_logit, axis=-1), jnp.sum(capped * onehot_f, axis=-1)), "mp"
    )
    nll = jnp.log(exp_total) - target_logit
    select = table_of_column[None, :, None] == jnp.arange(TABLES, dtype=jnp.int32)[None, None, :]
    counts = jnp.sum(jnp.where(select, fanout[:, None, :], 0), axis=-1).astype(fl)
    row_scale = 1.0 / (counts * row_total_count)
    ratio = capped / LOGIT_CAP
    d_logit = (
        (exp_logit / exp_total[:, :, None] - onehot_f)
        * row_scale[:, :, None]
        * (1.0 - ratio * ratio)
    ).astype(jnp.bfloat16)
    d_final_part = (
        jnp.einsum("rcv,cvd->rcd", d_logit, embed_table, preferred_element_type=fl) / width_root
    )
    table_grad = (
        jnp.einsum("rcv,rcd->cvd", d_logit, norm_final, preferred_element_type=fl) / width_root
    )
    d_final = lax.psum(d_final_part, "mp")
    back_full = norm_back_full(out_full, d_final, gain_final, rms_final)
    d_out_cols = lax.dynamic_slice_in_dim(back_full, mp_rank * part_width, part_width, 2).astype(
        jnp.bfloat16
    )
    d_out = cols_to_rows(d_out_cols)
    d_out_full = gather_features(d_out)
    d_hidden = jnp.einsum("rpd,df->rpf", d_out_full, w_down, preferred_element_type=fl)
    sigmoid_gate = jax.nn.sigmoid(gate_pre)
    d_gate = (d_hidden * up_proj * sigmoid_gate * (1.0 + gate_pre * (1.0 - sigmoid_gate))).astype(
        jnp.bfloat16
    )
    d_up = (d_hidden * gate_pre * sigmoid_gate).astype(jnp.bfloat16)
    d_norm_mlp = jnp.einsum("rpf,df->rpd", d_gate, w_gate, preferred_element_type=fl) + jnp.einsum(
        "rpf,df->rpd", d_up, w_up, preferred_element_type=fl
    )
    d_mid = (
        d_out.astype(fl)
        + norm_back_part(
            resid_mid, feature_sum(d_norm_mlp), own_part(gain_mlp), rms_mlp, model_width
        )
    ).astype(jnp.bfloat16)
    mid_grad_full = gather_features(d_mid)
    d_attn = jnp.einsum("rpd,dj->rpj", mid_grad_full, w_out, preferred_element_type=fl).astype(
        jnp.bfloat16
    )
    d_attn = d_attn.reshape(rows_here, col_count, local_heads, HS)
    d_prob = jnp.einsum("rqhe,rkhe->rhqk", d_attn, value_rows, preferred_element_type=fl)
    ratio_s = score / ATTN_CAP
    d_score = attn_prob * (d_prob - jnp.sum(attn_prob * d_prob, axis=-1, keepdims=True))
    d_scaled = (d_score * (1.0 - ratio_s * ratio_s) / math.sqrt(HS)).astype(jnp.bfloat16)
    d_query = jnp.einsum("rhqk,rkhe->rqhe", d_scaled, key_rows, preferred_element_type=fl)
    d_key = jnp.einsum("rhqk,rqhe->rkhe", d_scaled, queries, preferred_element_type=fl)
    d_value = jnp.einsum("rhqk,rqhe->rkhe", prob_b, d_attn, preferred_element_type=fl)
    d_qkv = (
        jnp.stack([d_query, d_key, d_value], axis=2)
        .reshape(rows_here, col_count, 3, head_cols)
        .astype(jnp.bfloat16)
    )
    d_norm_attn = jnp.einsum("rptx,dtx->rpd", d_qkv, w_qkv, preferred_element_type=fl)
    d_in = (
        d_mid.astype(fl)
        + norm_back_part(
            resid_in, feature_sum(d_norm_attn), own_part(gain_attn), rms_attn, model_width
        )
    ).astype(jnp.bfloat16)
    d_embed_rows = jnp.concatenate(
        [d_in[:, 1:], jnp.zeros((rows_here, 1, part_width), jnp.bfloat16)], axis=1
    )
    d_embed_cols = rows_to_cols(d_embed_rows)
    d_embed_full = gather_features(d_embed_cols)
    table_grad = table_grad + jnp.einsum(
        "rcv,rcd->cvd", onehot, d_embed_full, preferred_element_type=fl
    )
    qkv_term = jnp.einsum("rpd,rptx->dtx", norm_attn, d_qkv, preferred_element_type=fl).reshape(
        model_width, 3 * head_cols
    )
    out_term = jnp.einsum("rpd,rpj->dj", mid_grad_full, attn_out, preferred_element_type=fl)
    whole_terms = jnp.concatenate(
        [
            jnp.concatenate([qkv_term, out_term], axis=1),
            jnp.concatenate(
                [
                    jnp.einsum("rpd,rpf->df", norm_mlp, d_gate, preferred_element_type=fl),
                    jnp.einsum("rpd,rpf->df", norm_mlp, d_up, preferred_element_type=fl),
                    jnp.einsum("rpd,rpf->df", d_out_full, hidden, preferred_element_type=fl),
                ],
                axis=1,
            ),
        ],
        axis=1,
    )
    summed = lax.psum_scatter(whole_terms, "dp", scatter_dimension=0, tiled=True)
    ff_part = w_gate.shape[1]
    qkv_width = 3 * head_cols
    grad_qkv = summed[:, :qkv_width].reshape(summed.shape[0], 3, head_cols)
    grad_out = summed[:, qkv_width : qkv_width + head_cols]
    base = qkv_width + head_cols
    grad_gate = summed[:, base : base + ff_part]
    grad_up = summed[:, base + ff_part : base + 2 * ff_part]
    grad_down = summed[:, base + 2 * ff_part : base + 3 * ff_part]
    return (nll, table_grad, grad_qkv, grad_out, grad_gate, grad_up, grad_down)


def solution(mesh):
    return jax.shard_map(
        local,
        mesh=mesh,
        in_specs=(
            P(None, "dp"),
            P(),
            P("dp"),
            P("dp", "mp", None),
            P(),
            P(),
            P(),
            P(),
            P(None, None, "mp"),
            P(None, "mp"),
            P(None, "mp"),
            P(None, "mp"),
            P(None, "mp"),
        ),
        out_specs=(
            P(None, "dp"),
            P("dp", "mp", None),
            P("dp", None, "mp"),
            P("dp", "mp"),
            P("dp", "mp"),
            P("dp", "mp"),
            P("dp", "mp"),
        ),
        check_vma=False,
    )
```

profile of v0, /device:TPU:2, one launch (start us, length us, event | category | flops | bytes accessed | tf_op | source)
XLA Modules:
  0.0 726.3 jit_solution(7134462608592402723)
XLA Ops:
  8.0 2.4 convolution_bitcast_fusion
  10.4 44.1 %reduce-scatter.9.cloned.1.call-done = f32[128,2,128]{2,0,1:T(8,128)} async-done(((f32[128,2,1024]{2,0,1:T(8,128)}), f32[128,2,128]{2,0,1:T(8,128)}) %reduce-scatter.9.cloned.1.call-update) | async-done | bytes 131088 | tf_op jit(solution)/shard_map/reduce_scatter | solution.py:19
  54.5 0.9 convert_element_type.114
  56.1 10.0 %all-to-all-start = ((bf16[128,2,128]{2,1,0:T(2,128)(2,1)}), bf16[128,2,128]{2,1,0:T(2,128)(2,1)S(1)}, u32[]{:S(2)}, u32[]{:S(2)}) async-start(bf16[128,2,128]{2,1,0:T(2,128)(2,1)} %copy.114), calls=%async_computation.1 | async-start | bytes 131072 | tf_op jit(solution)/shard_map/all_to_all | solution.py:23
  67.7 8.4 %all-to-all-done = bf16[128,2,128]{2,1,0:T(2,128)(2,1)S(1)} async-done(((bf16[128,2,128]{2,1,0:T(2,128)(2,1)}), bf16[128,2,128]{2,1,0:T(2,128)(2,1)S(1)}, u32[]{:S(2)}, u32[]{:S(2)}) %all-to-all-start) | async-done | bytes 65568 | tf_op jit(solution)/shard_map/all_to_all | solution.py:23
  76.8 26.7 %all_gather.18 = bf16[4,64,1024]{2,1,0:T(8,128)(2,1)S(1)} all-gather(bf16[4,64,128]{2,1,0:T(8,128)(2,1)S(1)} %get-tuple-element.52), channel_id=1, replica_groups=mesh['dp'=32,'mp'=8] {'mp'}, dimensions={2}, use_global_device_ids=true | all-gather | bytes 589824 | tf_op jit(solution)/shard_map/all_gather | solution.py:15
  104.3 1.6 convolution_convert_fusion
  107.0 1.3 fusion.35
  108.4 34.5 %reduce-scatter.11.cloned.1.call-done = f32[4,64,128]{2,1,0:T(8,128)} async-done(((f32[4,64,1024]{2,1,0:T(8,128)}), f32[4,64,128]{2,1,0:T(8,128)}) %reduce-scatter.11.cloned.1.call-update) | async-done | bytes 131088 | tf_op jit(solution)/shard_map/reduce_scatter | solution.py:19
  142.9 0.9 add_convert_fusion
  143.8 26.9 %all_gather.19 = bf16[4,64,1024]{2,1,0:T(8,128)(2,1)S(1)} all-gather(bf16[4,64,128]{2,1,0:T(8,128)(2,1)S(1)} %add_convert_fusion), channel_id=1, replica_groups=mesh['dp'=32,'mp'=8] {'mp'}, dimensions={2}, use_global_device_ids=true | all-gather | bytes 589824 | tf_op jit(solution)/shard_map/all_gather | solution.py:15
  171.5 1.8 fusion.25
  173.3 0.8 copy-done.40
  174.1 2.5 multiply_convert_fusion.3
  176.7 1.4 fusion.18
  178.3 40.9 %reduce-scatter.13.cloned.1.call-done = f32[4,64,128]{2,1,0:T(8,128)} async-done(((f32[4,64,1024]{2,1,0:T(8,128)}), f32[4,64,128]{2,1,0:T(8,128)}) %reduce-scatter.13.cloned.1.call-update) | async-done | bytes 131088 | tf_op jit(solution)/shard_map/reduce_scatter | solution.py:19
  219.3 0.9 fusion.45
  220.9 10.0 %all-to-all-start.1 = ((bf16[4,64,128]{2,0,1:T(4,128)(2,1)}), bf16[4,64,128]{2,0,1:T(4,128)(2,1)S(1)}, u32[]{:S(2)}, u32[]{:S(2)}) async-start(bf16[4,64,128]{2,0,1:T(4,128)(2,1)} %copy.121), calls=%async_computation.4 | async-start | bytes 131072 | tf_op jit(solution)/shard_map/all_to_all | solution.py:27
  231.5 9.3 %all-to-all-done.1 = bf16[4,64,128]{2,0,1:T(4,128)(2,1)S(1)} async-done(((bf16[4,64,128]{2,0,1:T(4,128)(2,1)}), bf16[4,64,128]{2,0,1:T(4,128)(2,1)S(1)}, u32[]{:S(2)}, u32[]{:S(2)}) %all-to-all-start.1) | async-done | bytes 65568 | tf_op jit(solution)/shard_map/all_to_all | solution.py:27
  240.9 26.7 %all_gather.20 = bf16[128,2,1024]{2,0,1:T(8,128)(2,1)S(1)} all-gather(bf16[128,2,128]{2,0,1:T(8,128)(2,1)S(1)} %bitcast.144), channel_id=1, replica_groups=mesh['dp'=32,'mp'=8] {'mp'}, dimensions={2}, use_global_device_ids=true | all-gather | bytes 589824 | tf_op jit(solution)/shard_map/all_gather | solution.py:15
  268.3 1.6 fusion.63
  269.9 14.4 %psum.35 = f32[128,2]{0,1:T(2,128)S(1)} all-reduce(f32[128,2]{0,1:T(2,128)} %get-tuple-element.35), channel_id=1, replica_groups=mesh['dp'=32,'mp'=8] {'mp'}, use_global_device_ids=true, to_apply=%region_8.9 | all-reduce | flops 256 | bytes 2048 | tf_op jit(solution)/shard_map/psum | solution.py:136
  284.3 2.2 fusion.1
  286.6 1.1 convert_element_type.130
  287.8 76.1 %all-reduce.4.cloned.1.call-done = f32[128,2,1024]{2,0,1:T(8,128)} async-done(((f32[128,2,1024]{2,0,1:T(8,128)}), f32[128,2,1024]{2,0,1:T(8,128)}) %all-reduce.4.cloned.1.call-update) | async-done | bytes 1048592 | tf_op jit(solution)/shard_map/psum | solution.py:155
  363.9 1.6 multiply_reduce_fusion
  365.5 1.1 fusion.54
  366.6 19.4 %all_to_all.72 = bf16[128,2,128]{2,1,0:T(2,128)(2,1)S(1)} all-to-all(bf16[128,2,128]{2,1,0:T(2,128)(2,1)S(1)} %copy.124), channel_id=1, replica_groups=mesh['dp'=32,'mp'=8] {'dp'}, dimensions={0} | all-to-all | bytes 131072 | tf_op jit(solution)/shard_map/all_to_all | solution.py:23
  386.1 26.0 %all_gather.21 = bf16[4,64,1024]{2,1,0:T(8,128)(2,1)S(1)} all-gather(bf16[4,64,128]{2,1,0:T(8,128)(2,1)S(1)} %bitcast.138), channel_id=1, replica_groups=mesh['dp'=32,'mp'=8] {'mp'}, dimensions={2}, use_global_device_ids=true | all-gather | bytes 589824 | tf_op jit(solution)/shard_map/all_gather | solution.py:15
  412.1 1.9 multiply_convert_fusion.1
  414.8 1.4 convolution_add_fusion.1
  416.3 1.3 dynamic-slice_convert_fusion.1
  417.6 33.3 %reduce-scatter.15.cloned.1.call-done = f32[4,64,128]{2,1,0:T(8,128)} async-done(((f32[4,64,1024]{2,1,0:T(8,128)}), f32[4,64,128]{2,1,0:T(8,128)}) %reduce-scatter.15.cloned.1.call-update) | async-done | bytes 131088 | tf_op jit(solution)/shard_map/reduce_scatter | solution.py:19
  450.9 1.6 fusion.46
  452.5 18.0 %psum.38 = f32[4,64]{1,0:T(4,128)} all-reduce(f32[4,64]{1,0:T(4,128)} %fusion.46), channel_id=1, replica_groups=mesh['dp'=32,'mp'=8] {'mp'}, use_global_device_ids=true, to_apply=%region_16.17 | all-reduce | flops 256 | bytes 2048 | tf_op jit(solution)/shard_map/psum | solution.py:50
  470.5 1.1 fusion.61
  472.2 27.0 %all_gather.22 = bf16[4,64,1024]{2,1,0:T(8,128)(2,1)S(1)} all-gather(bf16[4,64,128]{2,1,0:T(8,128)(2,1)S(1)} %fusion.61), channel_id=1, replica_groups=mesh['dp'=32,'mp'=8] {'mp'}, dimensions={2}, use_global_device_ids=true | all-gather | bytes 589824 | tf_op jit(solution)/shard_map/all_gather | solution.py:15
  499.2 0.9 convolution_convert_fusion.5
  500.1 1.0 copy.166
  501.1 1.8 fusion.65
  502.9 1.8 convolution_convert_fusion.1
  504.7 1.6 convolution_convert_fusion.3
  506.3 2.2 convolution_convert_fusion.2
  508.5 1.0 copy.136
  509.5 1.0 copy.135
  510.7 2.6 convolution_bitcast_fusion.1
  513.6 2.7 bitcast_dynamic-update-slice_fusion.3
  516.2 2.0 fusion.2
  518.2 2.8 bitcast_dynamic-update-slice_fusion.2
  521.1 2.6 bitcast_dynamic-update-slice_fusion.1
  523.7 1.8 bitcast_dynamic-update-slice_fusion
  525.4 9.2 %copy.156 = f32[1024,2048]{1,0:T(8,128)} copy(f32[1024,2048]{0,1:T(8,128)} %bitcast_dynamic-update-slice_fusion) | data formatting | bytes 16777216
  534.7 0.9 dynamic-slice_convert_fusion
  535.7 1.5 convolution_multiply_fusion.1
  537.2 17.6 %reduce-scatter.17.cloned.1.call-done = f32[4,64,128]{2,1,0:T(8,128)} async-done(((f32[4,64,1024]{2,1,0:T(8,128)}), f32[4,64,128]{2,1,0:T(8,128)}) %reduce-scatter.17.cloned.1.call-update) | async-done | bytes 131088 | tf_op jit(solution)/shard_map/reduce_scatter | solution.py:19
  554.8 1.0 multiply_reduce_fusion.3
  555.9 17.3 %all-reduce.1 = (f32[128,2]{0,1:T(2,128)S(1)}, f32[4,64]{1,0:T(4,128)S(1)}) all-reduce(f32[128,2]{0,1:T(2,128)S(1)} %copy-done.36, f32[4,64]{1,0:T(4,128)S(1)} %get-tuple-element.39), channel_id=1, replica_groups=mesh['dp'=32,'mp'=8] {'mp'}, use_global_device_ids=true, to_apply=%region_10.11 | all-reduce | flops 512 | bytes 4096 | tf_op jit(solution)/shard_map/psum | solution.py:136
  574.1 10.0 %all-to-all-start.3 = ((bf16[4,64,128]{2,0,1:T(4,128)(2,1)}), bf16[4,64,128]{2,0,1:T(4,128)(2,1)S(1)}, u32[]{:S(2)}, u32[]{:S(2)}) async-start(bf16[4,64,128]{2,0,1:T(4,128)(2,1)} %concatenate.12.clone), calls=%async_computation.8 | async-start | bytes 131072 | tf_op jit(solution)/shard_map/all_to_all | solution.py:27
  584.6 9.4 %all-to-all-done.3 = bf16[4,64,128]{2,0,1:T(4,128)(2,1)S(1)} async-done(((bf16[4,64,128]{2,0,1:T(4,128)(2,1)}), bf16[4,64,128]{2,0,1:T(4,128)(2,1)S(1)}, u32[]{:S(2)}, u32[]{:S(2)}) %all-to-all-start.3) | async-done | bytes 65568 | tf_op jit(solution)/shard_map/all_to_all | solution.py:27
  594.0 28.0 %all_gather.23 = bf16[128,2,1024]{2,0,1:T(8,128)(2,1)S(1)} all-gather(bf16[128,2,128]{2,0,1:T(8,128)(2,1)S(1)} %bitcast.145), channel_id=1, replica_groups=mesh['dp'=32,'mp'=8] {'mp'}, dimensions={2}, use_global_device_ids=true | all-gather | bytes 589824 | tf_op jit(solution)/shard_map/all_gather | solution.py:15
  622.0 2.5 convolution_add_fusion
  624.5 90.4 %reduce-scatter.19.cloned.1.call-done = f32[32,2048]{1,0:T(8,128)} async-done(((f32[1024,2048]{1,0:T(8,128)}), f32[32,2048]{1,0:T(8,128)}) %reduce-scatter.19.cloned.1.call-update) | async-done | bytes 262160
  716.6 1.3 slice.51
  717.9 1.6 fusion.94
  (137 shorter events, 14.1 us)
Async XLA Ops:
  7.2 169.5 %copy-start = (bf16[1024,512]{1,0:T(8,128)(2,1)S(1)}, bf16[1024,512]{1,0:T(8,128)(2,1)}, u32[]{:S(2)}) copy-start(bf16[1024,512]{1,0:T(8,128)(2,1)} %param.25) | copy-start | bytes 3145732
  7.2 99.8 %copy-start.6 = (bf16[1024,128]{1,0:T(8,128)(2,1)S(1)}, bf16[1024,128]{1,0:T(8,128)(2,1)}, u32[]{:S(2)}) copy-start(bf16[1024,128]{1,0:T(8,128)(2,1)} %param.22) | copy-start | bytes 786436
  7.2 101.1 %copy-start.35 = (bf16[1024]{0:T(1024)(128)(2,1)S(1)}, bf16[1024]{0:T(1024)(128)(2,1)}, u32[]{:S(2)}) copy-start(bf16[1024]{0:T(1024)(128)(2,1)} %param.19) | copy-start | bytes 6148
  7.2 47.3 %reduce-scatter.9.cloned.1.call-start = ((), (), s32[]{:S(2)}) async-start(), calls=%async_computation.10 | async-start | bytes 1179648 | tf_op jit(solution)/shard_map/reduce_scatter | solution.py:19
  56.1 20.0 %all-to-all-start = ((bf16[128,2,128]{2,1,0:T(2,128)(2,1)}), bf16[128,2,128]{2,1,0:T(2,128)(2,1)S(1)}, u32[]{:S(2)}, u32[]{:S(2)}) async-start(bf16[128,2,128]{2,1,0:T(2,128)(2,1)} %copy.114), calls=%async_computation.1 | async-start | bytes 131072 | tf_op jit(solution)/shard_map/all_to_all | solution.py:23
  66.1 76.7 %reduce-scatter.11.cloned.1.call-start = ((), (), s32[]{:S(2)}) async-start(), calls=%async_computation.11 | async-start | bytes 1179648 | tf_op jit(solution)/shard_map/reduce_scatter | solution.py:19
  66.9 39.3 %copy-start.30 = (f32[1024]{0:T(1024)}, f32[1024]{0:T(1024)S(1)}, u32[]{:S(2)}) copy-start(f32[1024]{0:T(1024)S(1)} %convert_element_type.117) | copy-start | bytes 12292
  67.7 76.2 %copy-start.28 = (pred[64,64]{0,1:T(8,128)(4,1)}, pred[64,64]{0,1:T(8,128)(4,1)S(1)}, u32[]{:S(2)}) copy-start(pred[64,64]{0,1:T(8,128)(4,1)S(1)} %iota_compare_fusion.3) | copy-start | bytes 12292
  104.3 1.9 copy-start.25
  106.1 36.8 %copy-start.21 = (bf16[4,64,1,128]{1,3,0,2:T(8,128)(2,1)}, bf16[4,64,1,128]{1,3,0,2:T(8,128)(2,1)S(1)}, u32[]{:S(2)}) copy-start(bf16[4,64,1,128]{1,3,0,2:T(8,128)(2,1)S(1)} %copy.165) | copy-start | bytes 196612
  106.2 36.7 %copy-start.13 = (bf16[4,64,2,64]{3,2,1,0:T(2,128)(2,1)}, bf16[4,64,2,64]{3,2,1,0:T(2,128)(2,1)S(1)}, u32[]{:S(2)}) copy-start(bf16[4,64,2,64]{3,2,1,0:T(2,128)(2,1)S(1)} %reshape_squeeze.9) | copy-start | bytes 196612
  106.4 36.5 %copy-start.22 = (bf16[4,64,1,128]{1,3,0,2:T(8,128)(2,1)}, bf16[4,64,1,128]{1,3,0,2:T(8,128)(2,1)S(1)}, u32[]{:S(2)}) copy-start(bf16[4,64,1,128]{1,3,0,2:T(8,128)(2,1)S(1)} %copy.164) | copy-start | bytes 196612
  106.7 1.6 copy-start.38
  106.7 64.0 %copy-start.39 = (f32[4,2,64]{2,1,0:T(2,128)}, f32[4,2,64]{2,1,0:T(2,128)S(1)}, u32[]{:S(2)}) copy-start(f32[4,2,64]{2,1,0:T(2,128)S(1)} %get-tuple-element.59) | copy-start | bytes 6148
  106.9 35.9 %copy-start.14 = (bf16[4,2,64,64]{3,2,1,0:T(8,128)(2,1)}, bf16[4,2,64,64]{3,2,1,0:T(8,128)(2,1)S(1)}, u32[]{:S(2)}) copy-start(bf16[4,2,64,64]{3,2,1,0:T(8,128)(2,1)S(1)} %convolution_convert_fusion.4) | copy-start | bytes 196612
  108.3 111.0 %reduce-scatter.13.cloned.1.call-start = ((), (), s32[]{:S(2)}) async-start(), calls=%async_computation.12 | async-start | bytes 1179648 | tf_op jit(solution)/shard_map/reduce_scatter | solution.py:19
  108.4 69.7 %copy-start.31 = (f32[1024]{0:T(1024)}, f32[1024]{0:T(1024)S(1)}, u32[]{:S(2)}) copy-start(f32[1024]{0:T(1024)S(1)} %convert_element_type.126) | copy-start | bytes 12292
  171.5 6.6 copy-start.23
  171.5 6.6 copy-start.34
  171.5 6.6 copy-start.37
  171.5 6.7 copy-start.27
  171.5 96.8 %copy-start.1 = (bf16[2,128,1024]{2,1,0:T(8,128)(2,1)S(1)}, bf16[2,128,1024]{2,1,0:T(8,128)(2,1)}, u32[]{:S(2)}) copy-start(bf16[2,128,1024]{2,1,0:T(8,128)(2,1)} %param.16) | copy-start | bytes 1572868
  173.3 0.8 copy-start.40
  176.7 64.2 %copy-start.7 = (bf16[4,64,512]{2,1,0:T(8,128)(2,1)}, bf16[4,64,512]{2,1,0:T(8,128)(2,1)S(1)}, u32[]{:S(2)}) copy-start(bf16[4,64,512]{2,1,0:T(8,128)(2,1)S(1)} %get-tuple-element.61) | copy-start | bytes 786436
  220.9 20.0 %all-to-all-start.1 = ((bf16[4,64,128]{2,0,1:T(4,128)(2,1)}), bf16[4,64,128]{2,0,1:T(4,128)(2,1)S(1)}, u32[]{:S(2)}, u32[]{:S(2)}) async-start(bf16[4,64,128]{2,0,1:T(4,128)(2,1)} %copy.121), calls=%async_computation.4 | async-start | bytes 131072 | tf_op jit(solution)/shard_map/all_to_all | solution.py:27
  230.9 133.0 %all-reduce.4.cloned.1.call-start = ((), (), s32[]{:S(2)}) async-start(), calls=%async_computation.13 | async-start | bytes 2097152 | tf_op jit(solution)/shard_map/psum | solution.py:155
  268.3 1.6 copy-start.32
  286.6 164.3 %reduce-scatter.15.cloned.1.call-start = ((), (), s32[]{:S(2)}) async-start(), calls=%async_computation.14 | async-start | bytes 1179648 | tf_op jit(solution)/shard_map/reduce_scatter | solution.py:19
  363.9 50.2 %copy-start.4 = (bf16[1024,512]{1,0:T(8,128)(2,1)S(1)}, bf16[1024,512]{1,0:T(8,128)(2,1)}, u32[]{:S(2)}) copy-start(bf16[1024,512]{1,0:T(8,128)(2,1)} %param.23) | copy-start | bytes 3145732
  363.9 51.0 %copy-start.5 = (bf16[1024,512]{1,0:T(8,128)(2,1)S(1)}, bf16[1024,512]{1,0:T(8,128)(2,1)}, u32[]{:S(2)}) copy-start(bf16[1024,512]{1,0:T(8,128)(2,1)} %param.24) | copy-start | bytes 3145732
  386.0 28.0 %copy-start.11 = (bf16[32,4,2,128]{3,2,0,1:T(2,128)(2,1)}, bf16[32,4,2,128]{3,2,0,1:T(2,128)(2,1)S(1)}, u32[]{:S(2)}) copy-start(bf16[32,4,2,128]{3,2,0,1:T(2,128)(2,1)S(1)} %copy.125) | copy-start | bytes 196612
  412.1 58.4 %copy-start.2 = (bf16[4,64,1024]{2,1,0:T(8,128)(2,1)}, bf16[4,64,1024]{2,1,0:T(8,128)(2,1)S(1)}, u32[]{:S(2)}) copy-start(bf16[4,64,1024]{2,1,0:T(8,128)(2,1)S(1)} %all_gather.21) | copy-start | bytes 1572868
  414.0 0.7 copy-start.15
  414.0 0.8 copy-start.18
  416.3 138.5 %reduce-scatter.17.cloned.1.call-start = ((), (), s32[]{:S(2)}) async-start(), calls=%async_computation.15 | async-start | bytes 1179648 | tf_op jit(solution)/shard_map/reduce_scatter | solution.py:19
  471.6 0.6 copy-start.9
  510.5 2.7 copy-start.16
  510.7 2.6 copy-start.17
  513.3 10.3 %copy-start.8 = (bf16[4,64,512]{2,1,0:T(8,128)(2,1)S(1)}, bf16[4,64,512]{2,1,0:T(8,128)(2,1)}, u32[]{:S(2)}) copy-start(bf16[4,64,512]{2,1,0:T(8,128)(2,1)} %copy-done.7) | copy-start | bytes 786436
  513.3 201.6 %reduce-scatter.19.cloned.1.call-start = ((), (), s32[]{:S(2)}) async-start(), calls=%async_computation.16 | async-start | bytes 8650752
  513.6 7.5 %copy-start.19 = (bf16[4,64,512]{2,1,0:T(8,128)(2,1)S(1)}, bf16[4,64,512]{2,1,0:T(8,128)(2,1)}, u32[]{:S(2)}) copy-start(bf16[4,64,512]{2,1,0:T(8,128)(2,1)} %copy-done.18) | copy-start | bytes 786436
  513.6 10.1 %copy-start.3 = (bf16[4,64,1024]{2,1,0:T(8,128)(2,1)S(1)}, bf16[4,64,1024]{2,1,0:T(8,128)(2,1)}, u32[]{:S(2)}) copy-start(bf16[4,64,1024]{2,1,0:T(8,128)(2,1)} %copy-done.2) | copy-start | bytes 1572868
  534.6 0.9 copy-start.26
  534.6 1.0 copy-start.24
  534.6 1.1 copy-start.20
  534.6 1.1 copy-start.29
  534.6 1.1 copy-start.33
  534.7 21.2 %copy-start.36 = (f32[128,2]{0,1:T(2,128)S(1)}, f32[128,2]{0,1:T(2,128)}, u32[]{:S(2)}) copy-start(f32[128,2]{0,1:T(2,128)} %get-tuple-element.36) | copy-start | bytes 3076
  534.7 38.5 %copy-start.10 = (bf16[4,64,128]{2,1,0:T(8,128)(2,1)S(1)}, bf16[4,64,128]{2,1,0:T(8,128)(2,1)}, u32[]{:S(2)}) copy-start(bf16[4,64,128]{2,1,0:T(8,128)(2,1)} %copy-done.9) | copy-start | bytes 196612
  534.7 38.5 %copy-start.12 = (f32[4,64,128]{2,1,0:T(8,128)S(1)}, f32[4,64,128]{2,1,0:T(8,128)}, u32[]{:S(2)}) copy-start(f32[4,64,128]{2,1,0:T(8,128)} %get-tuple-element.51) | copy-start | bytes 393220
  574.1 19.9 %all-to-all-start.3 = ((bf16[4,64,128]{2,0,1:T(4,128)(2,1)}), bf16[4,64,128]{2,0,1:T(4,128)(2,1)S(1)}, u32[]{:S(2)}, u32[]{:S(2)}) async-start(bf16[4,64,128]{2,0,1:T(4,128)(2,1)} %concatenate.12.clone), calls=%async_computation.8 | async-start | bytes 131072 | tf_op jit(solution)/shard_map/all_to_all | solution.py:27
Sparse Core Ops, SparseCore 0:
  11.1 43.3 reduce-scatter.8
  108.4 34.4 reduce-scatter.10
  178.3 40.9 reduce-scatter.12
  286.7 77.0 all-reduce.3
  416.4 34.4 reduce-scatter.14
  513.4 41.3 reduce-scatter.16
  559.2 155.6 reduce-scatter.18
where the time goes:
time: 728 us; the launch traced here: 726 us
  waiting for transfers between devices  364 us (50%)
  blocking collectives  230 us (32%)
  matrix products  46 us (6%)
  starting transfers between devices  30.4 us (4%)
  local copies, waits for them, and re-layouts  22.4 us (3%)
  other arithmetic  18.3 us (3%)
  between operations  14.7 us (2%)
    reduce_scatter x5, waiting for transfers between devices, feature_sum(): return lax.psum_scatter(term, 'mp', scatter_dimension=2, tiled=True)  170 us
    all_gather x6, blocking collectives, gather_features(): return lax.all_gather(values, 'mp', axis=2, tiled=True)  161 us
    unnamed x8, waiting for transfers between devices  90.5 us
    psum x1, waiting for transfers between devices, local(): d_final = lax.psum(d_final_part, 'mp')  76.1 us
    psum x2, blocking collectives, local(): lax.psum((jnp.sum(exp_logit, axis=-1), jnp.sum(capped * onehot_f, axis=-1...  31.7 us
    all_to_all x2, starting transfers between devices, rows_to_cols(): return lax.all_to_all(values, 'dp', split_axis=1, concat_axis=0, tiled=True)  20 us
    all_to_all x1, blocking collectives, cols_to_rows(): return lax.all_to_all(values, 'dp', split_axis=0, concat_axis=1, tiled=True)  19.4 us
    all_to_all x2, waiting for transfers between devices, rows_to_cols(): return lax.all_to_all(values, 'dp', split_axis=1, concat_axis=0, tiled=True)  18.7 us
  transfers between devices with their start and end apart: 10, of which 10 were waited for; matrix products, arithmetic and copies ran while one was open for 5% of the time, Pallas kernels for 0%

commit v1 on v0

--- a/solution.py
+++ b/solution.py
@@ -24,7 +24,15 @@
 
 
 def rows_to_cols(values):
-    return lax.all_to_all(values, "dp", split_axis=1, concat_axis=0, tiled=True)
+    return jnp.concatenate(
+        jax.lax.all_to_all(
+            jnp.stack(jnp.split(values, jax.lax.axis_size("dp"), axis=1)),
+            axis_name="dp",
+            split_axis=0,
+            concat_axis=0,
+        ),
+        axis=0,
+    )
 
 
 def rms_of(values):

time: 728 us -> 749 us (1.029)
  local copies, waits for them, and re-layouts: 22.4 us -> 56.7 us
  waiting for transfers between devices: 364 us -> 352 us
    unnamed x86 -> x145, local copies, waits for them, and re-layouts: 12 us -> 47.5 us
    unnamed x8, waiting for transfers between devices: 90.5 us -> 78.4 us
  transfers between devices with their start and end apart: 10 -> 10, of which waited for: 10 -> 10; matrix products, arithmetic and copies ran while one was open for 5% -> 7% of each run, Pallas kernels for 0% -> 0%
where the time goes in v1:
time: 749 us; the launch traced here: 748 us
  waiting for transfers between devices  352 us (47%)
  blocking collectives  230 us (31%)
  local copies, waits for them, and re-layouts  56.7 us (8%)
  matrix products  45.5 us (6%)
  starting transfers between devices  30.1 us (4%)
  other arithmetic  18.6 us (2%)
  between operations  14.7 us (2%)
    reduce_scatter x5, waiting for transfers between devices, feature_sum(): return lax.psum_scatter(term, 'mp', scatter_dimension=2, tiled=True)  171 us
    all_gather x6, blocking collectives, gather_features(): return lax.all_gather(values, 'mp', axis=2, tiled=True)  161 us
    unnamed x8, waiting for transfers between devices  78.4 us
    psum x1, waiting for transfers between devices, local(): d_final = lax.psum(d_final_part, 'mp')  76.1 us
    unnamed x145, local copies, waits for them, and re-layouts  47.5 us
    psum x2, blocking collectives, local(): lax.psum((jnp.sum(exp_logit, axis=-1), jnp.sum(capped * onehot_f, axis=-1...  31.8 us
    all_to_all x2, starting transfers between devices, rows_to_cols(): jax.lax.all_to_all(jnp.stack(jnp.split(values, jax.lax.axis_size('dp'), a...  19.6 us
    all_to_all x1, blocking collectives, cols_to_rows(): return lax.all_to_all(values, 'dp', split_axis=0, concat_axis=1, tiled=True)  19.4 us
  transfers between devices with their start and end apart: 10, of which 10 were waited for; matrix products, arithmetic and copies ran while one was open for 7% of the time, Pallas kernels for 0%

profile of v1, /device:TPU:2, one launch (start us, length us, event | category | flops | bytes accessed | tf_op | source)
XLA Modules:
  0.0 747.6 jit_solution(2347491525594593743)
XLA Ops:
  7.3 0.8 broadcast_subtract_fusion
  8.0 2.4 convolution_bitcast_fusion
  10.4 44.1 %reduce-scatter.9.cloned.1.call-done = f32[128,2,128]{2,0,1:T(8,128)} async-done(((f32[128,2,1024]{2,0,1:T(8,128)}), f32[128,2,128]{2,0,1:T(8,128)}) %reduce-scatter.9.cloned.1.call-update) | async-done | bytes 131088 | tf_op jit(solution)/shard_map/reduce_scatter | solution.py:19
  54.5 0.9 convert_element_type.114
  56.1 10.0 %all-to-all-start = ((bf16[128,2,128]{2,1,0:T(2,128)(2,1)}), bf16[128,2,128]{2,1,0:T(2,128)(2,1)S(1)}, u32[]{:S(2)}, u32[]{:S(2)}) async-start(bf16[128,2,128]{2,1,0:T(2,128)(2,1)} %copy.112), calls=%async_computation.1 | async-start | bytes 131072 | tf_op jit(solution)/shard_map/all_to_all | solution.py:23
  67.7 8.4 %all-to-all-done = bf16[128,2,128]{2,1,0:T(2,128)(2,1)S(1)} async-done(((bf16[128,2,128]{2,1,0:T(2,128)(2,1)}), bf16[128,2,128]{2,1,0:T(2,128)(2,1)S(1)}, u32[]{:S(2)}, u32[]{:S(2)}) %all-to-all-start) | async-done | bytes 65568 | tf_op jit(solution)/shard_map/all_to_all | solution.py:23
  76.2 26.7 %all_gather.18 = bf16[4,64,1024]{2,1,0:T(8,128)(2,1)S(1)} all-gather(bf16[4,64,128]{2,1,0:T(8,128)(2,1)S(1)} %pad_maximum_fusion.2), channel_id=1, replica_groups=mesh['dp'=32,'mp'=8] {'mp'}, dimensions={2}, use_global_device_ids=true | all-gather | bytes 589824 | tf_op jit(solution)/shard_map/all_gather | solution.py:15
  103.7 1.6 convolution_convert_fusion
  106.4 1.3 fusion.35
  107.8 34.4 %reduce-scatter.11.cloned.1.call-done = f32[4,64,128]{2,1,0:T(8,128)} async-done(((f32[4,64,1024]{2,1,0:T(8,128)}), f32[4,64,128]{2,1,0:T(8,128)}) %reduce-scatter.11.cloned.1.call-update) | async-done | bytes 131088 | tf_op jit(solution)/shard_map/reduce_scatter | solution.py:19
  142.2 0.9 fusion.45
  143.1 26.9 %all_gather.19 = bf16[4,64,1024]{2,1,0:T(8,128)(2,1)S(1)} all-gather(bf16[4,64,128]{2,1,0:T(8,128)(2,1)S(1)} %fusion.45), channel_id=1, replica_groups=mesh['dp'=32,'mp'=8] {'mp'}, dimensions={2}, use_global_device_ids=true | all-gather | bytes 589824 | tf_op jit(solution)/shard_map/all_gather | solution.py:15
  170.9 1.8 fusion.25
  172.7 2.7 multiply_convert_fusion.3
  175.4 1.4 fusion.18
  177.1 41.0 %reduce-scatter.13.cloned.1.call-done = f32[4,64,128]{2,1,0:T(8,128)} async-done(((f32[4,64,1024]{2,1,0:T(8,128)}), f32[4,64,128]{2,1,0:T(8,128)}) %reduce-scatter.13.cloned.1.call-update) | async-done | bytes 131088 | tf_op jit(solution)/shard_map/reduce_scatter | solution.py:19
  218.1 0.9 fusion.50
  237.7 9.9 %all-to-all-start.1 = ((bf16[32,4,2,128]{3,2,1,0:T(2,128)(2,1)}), bf16[32,4,2,128]{3,2,1,0:T(2,128)(2,1)S(1)}, u32[]{:S(2)}, u32[]{:S(2)}) async-start(bf16[32,4,2,128]{3,2,1,0:T(2,128)(2,1)} %constant_dynamic-update-slice_fusion), calls=%async_computation.4 | async-start | bytes 131072 | tf_op jit(solution)/shard_map/all_to_all | solution.py:28
  248.2 9.3 %all-to-all-done.1 = bf16[32,4,2,128]{3,2,1,0:T(2,128)(2,1)S(1)} async-done(((bf16[32,4,2,128]{3,2,1,0:T(2,128)(2,1)}), bf16[32,4,2,128]{3,2,1,0:T(2,128)(2,1)S(1)}, u32[]{:S(2)}, u32[]{:S(2)}) %all-to-all-start.1) | async-done | bytes 65568 | tf_op jit(solution)/shard_map/all_to_all | solution.py:28
  257.5 26.7 %all_gather.20 = bf16[128,2,1024]{2,0,1:T(8,128)(2,1)S(1)} all-gather(bf16[128,2,128]{2,0,1:T(8,128)(2,1)S(1)} %copy.119), channel_id=1, replica_groups=mesh['dp'=32,'mp'=8] {'mp'}, dimensions={2}, use_global_device_ids=true | all-gather | bytes 589824 | tf_op jit(solution)/shard_map/all_gather | solution.py:15
  285.0 1.6 fusion.65
  286.6 14.4 %psum.35 = f32[128,2]{0,1:T(2,128)S(1)} all-reduce(f32[128,2]{0,1:T(2,128)} %get-tuple-element.35), channel_id=1, replica_groups=mesh['dp'=32,'mp'=8] {'mp'}, use_global_device_ids=true, to_apply=%region_8.9 | all-reduce | flops 256 | bytes 2048 | tf_op jit(solution)/shard_map/psum | solution.py:144
  301.0 2.2 fusion.1
  303.3 1.1 convert_element_type.130
  304.4 76.1 %all-reduce.4.cloned.1.call-done = f32[128,2,1024]{2,0,1:T(8,128)} async-done(((f32[128,2,1024]{2,0,1:T(8,128)}), f32[128,2,1024]{2,0,1:T(8,128)}) %all-reduce.4.cloned.1.call-update) | async-done | bytes 1048592 | tf_op jit(solution)/shard_map/psum | solution.py:163
  380.5 1.6 multiply_reduce_fusion
  382.1 1.1 fusion.56
  383.3 19.4 %all_to_all.46 = bf16[128,2,128]{2,1,0:T(2,128)(2,1)S(1)} all-to-all(bf16[128,2,128]{2,1,0:T(2,128)(2,1)S(1)} %copy.121), channel_id=1, replica_groups=mesh['dp'=32,'mp'=8] {'dp'}, dimensions={0} | all-to-all | bytes 131072 | tf_op jit(solution)/shard_map/all_to_all | solution.py:23
  402.7 26.0 %all_gather.21 = bf16[4,64,1024]{2,1,0:T(8,128)(2,1)S(1)} all-gather(bf16[4,64,128]{2,1,0:T(8,128)(2,1)S(1)} %bitcast.389), channel_id=1, replica_groups=mesh['dp'=32,'mp'=8] {'mp'}, dimensions={2}, use_global_device_ids=true | all-gather | bytes 589824 | tf_op jit(solution)/shard_map/all_gather | solution.py:15
  428.7 1.9 multiply_convert_fusion.1
  431.5 1.4 convolution_add_fusion.1
  433.0 1.3 dynamic-slice_convert_fusion.1
  434.2 33.3 %reduce-scatter.15.cloned.1.call-done = f32[4,64,128]{2,1,0:T(8,128)} async-done(((f32[4,64,1024]{2,1,0:T(8,128)}), f32[4,64,128]{2,1,0:T(8,128)}) %reduce-scatter.15.cloned.1.call-update) | async-done | bytes 131088 | tf_op jit(solution)/shard_map/reduce_scatter | solution.py:19
  467.5 1.6 fusion.51
  469.1 18.0 %psum.38 = f32[4,64]{1,0:T(4,128)} all-reduce(f32[4,64]{1,0:T(4,128)} %fusion.51), channel_id=1, replica_groups=mesh['dp'=32,'mp'=8] {'mp'}, use_global_device_ids=true, to_apply=%region_16.17 | all-reduce | flops 256 | bytes 2048 | tf_op jit(solution)/shard_map/psum | solution.py:58
  487.1 1.1 fusion.63
  488.9 26.8 %all_gather.22 = bf16[4,64,1024]{2,1,0:T(8,128)(2,1)S(1)} all-gather(bf16[4,64,128]{2,1,0:T(8,128)(2,1)S(1)} %fusion.63), channel_id=1, replica_groups=mesh['dp'=32,'mp'=8] {'mp'}, dimensions={2}, use_global_device_ids=true | all-gather | bytes 589824 | tf_op jit(solution)/shard_map/all_gather | solution.py:15
  516.1 1.8 fusion.67
  517.8 1.6 convolution_convert_fusion.3
  519.5 2.2 convolution_convert_fusion.2
  521.7 1.8 convolution_convert_fusion.1
  523.6 1.0 copy.132
  524.6 1.0 copy.133
  525.7 2.6 convolution_bitcast_fusion.1
  528.6 2.6 bitcast_dynamic-update-slice_fusion.3
  531.2 2.0 fusion.2
  533.2 2.8 bitcast_dynamic-update-slice_fusion.2
  536.0 2.6 bitcast_dynamic-update-slice_fusion.1
  538.6 1.8 bitcast_dynamic-update-slice_fusion
  540.4 9.2 %copy.152 = f32[1024,2048]{1,0:T(8,128)} copy(f32[1024,2048]{0,1:T(8,128)} %bitcast_dynamic-update-slice_fusion) | data formatting | bytes 16777216
  549.7 0.8 dynamic-slice_convert_fusion
  550.5 1.5 convolution_multiply_fusion.1
  552.0 17.9 %reduce-scatter.17.cloned.1.call-done = f32[4,64,128]{2,1,0:T(8,128)} async-done(((f32[4,64,1024]{2,1,0:T(8,128)}), f32[4,64,128]{2,1,0:T(8,128)}) %reduce-scatter.17.cloned.1.call-update) | async-done | bytes 131088 | tf_op jit(solution)/shard_map/reduce_scatter | solution.py:19
  569.9 1.0 fusion.46
  570.9 17.4 %all-reduce.1 = (f32[128,2]{0,1:T(2,128)S(1)}, f32[4,64]{1,0:T(4,128)S(1)}) all-reduce(f32[128,2]{0,1:T(2,128)S(1)} %copy-done.35, f32[4,64]{1,0:T(4,128)S(1)} %fusion.46), channel_id=1, replica_groups=mesh['dp'=32,'mp'=8] {'mp'}, use_global_device_ids=true, to_apply=%region_10.11 | all-reduce | flops 512 | bytes 4096 | tf_op jit(solution)/shard_map/psum | solution.py:144
  588.3 1.1 fusion.64
  608.1 9.7 %all-to-all-start.3 = ((bf16[32,4,2,128]{3,2,1,0:T(2,128)(2,1)}), bf16[32,4,2,128]{3,2,1,0:T(2,128)(2,1)S(1)}, u32[]{:S(2)}, u32[]{:S(2)}) async-start(bf16[32,4,2,128]{3,2,1,0:T(2,128)(2,1)} %constant_dynamic-update-slice_fusion.32), calls=%async_computation.8 | async-start | bytes 131072 | tf_op jit(solution)/shard_map/all_to_all | solution.py:28
  618.4 9.4 %all-to-all-done.3 = bf16[32,4,2,128]{3,2,1,0:T(2,128)(2,1)S(1)} async-done(((bf16[32,4,2,128]{3,2,1,0:T(2,128)(2,1)}), bf16[32,4,2,128]{3,2,1,0:T(2,128)(2,1)S(1)}, u32[]{:S(2)}, u32[]{:S(2)}) %all-to-all-start.3) | async-done | bytes 65568 | tf_op jit(solution)/shard_map/all_to_all | solution.py:28
  627.8 27.5 %all_gather.23 = bf16[128,2,1024]{2,0,1:T(8,128)(2,1)S(1)} all-gather(bf16[128,2,128]{2,0,1:T(8,128)(2,1)S(1)} %copy.134), channel_id=1, replica_groups=mesh['dp'=32,'mp'=8] {'mp'}, dimensions={2}, use_global_device_ids=true | all-gather | bytes 589824 | tf_op jit(solution)/shard_map/all_gather | solution.py:15
  655.3 2.5 convolution_add_fusion
  657.8 78.3 %reduce-scatter.19.cloned.1.call-done = f32[32,2048]{1,0:T(8,128)} async-done(((f32[1024,2048]{1,0:T(8,128)}), f32[32,2048]{1,0:T(8,128)}) %reduce-scatter.19.cloned.1.call-update) | async-done | bytes 262160
  736.2 0.8 slice.76
  737.8 1.6 fusion.96
  739.4 1.3 slice.77
  (194 shorter events, 47.9 us)
Async XLA Ops:
  7.2 168.2 %copy-start = (bf16[1024,512]{1,0:T(8,128)(2,1)S(1)}, bf16[1024,512]{1,0:T(8,128)(2,1)}, u32[]{:S(2)}) copy-start(bf16[1024,512]{1,0:T(8,128)(2,1)} %param.25) | copy-start | bytes 3145732
  7.2 99.2 %copy-start.6 = (bf16[1024,128]{1,0:T(8,128)(2,1)S(1)}, bf16[1024,128]{1,0:T(8,128)(2,1)}, u32[]{:S(2)}) copy-start(bf16[1024,128]{1,0:T(8,128)(2,1)} %param.22) | copy-start | bytes 786436
  7.2 100.6 %copy-start.34 = (bf16[1024]{0:T(1024)(128)(2,1)S(1)}, bf16[1024]{0:T(1024)(128)(2,1)}, u32[]{:S(2)}) copy-start(bf16[1024]{0:T(1024)(128)(2,1)} %param.19) | copy-start | bytes 6148
  7.2 47.3 %reduce-scatter.9.cloned.1.call-start = ((), (), s32[]{:S(2)}) async-start(), calls=%async_computation.10 | async-start | bytes 1179648 | tf_op jit(solution)/shard_map/reduce_scatter | solution.py:19
  56.1 20.0 %all-to-all-start = ((bf16[128,2,128]{2,1,0:T(2,128)(2,1)}), bf16[128,2,128]{2,1,0:T(2,128)(2,1)S(1)}, u32[]{:S(2)}, u32[]{:S(2)}) async-start(bf16[128,2,128]{2,1,0:T(2,128)(2,1)} %copy.112), calls=%async_computation.1 | async-start | bytes 131072 | tf_op jit(solution)/shard_map/all_to_all | solution.py:23
  66.1 76.0 %reduce-scatter.11.cloned.1.call-start = ((), (), s32[]{:S(2)}) async-start(), calls=%async_computation.11 | async-start | bytes 1179648 | tf_op jit(solution)/shard_map/reduce_scatter | solution.py:19
  66.9 38.6 %copy-start.29 = (f32[1024]{0:T(1024)}, f32[1024]{0:T(1024)S(1)}, u32[]{:S(2)}) copy-start(f32[1024]{0:T(1024)S(1)} %convert_element_type.117) | copy-start | bytes 12292
  67.7 74.5 %copy-start.27 = (pred[64,64]{0,1:T(8,128)(4,1)}, pred[64,64]{0,1:T(8,128)(4,1)S(1)}, u32[]{:S(2)}) copy-start(pred[64,64]{0,1:T(8,128)(4,1)S(1)} %iota_compare_fusion.3) | copy-start | bytes 12292
  103.7 69.0 %copy-start.23 = (f32[4,64]{1,0:T(4,128)}, f32[4,64]{1,0:T(4,128)S(1)}, u32[]{:S(2)}) copy-start(f32[4,64]{1,0:T(4,128)S(1)} %get-tuple-element.50) | copy-start | bytes 3076
  105.5 0.7 copy-start.20
  105.6 36.6 %copy-start.21 = (bf16[4,64,1,128]{1,3,0,2:T(8,128)(2,1)}, bf16[4,64,1,128]{1,3,0,2:T(8,128)(2,1)S(1)}, u32[]{:S(2)}) copy-start(bf16[4,64,1,128]{1,3,0,2:T(8,128)(2,1)S(1)} %copy.160) | copy-start | bytes 196612
  105.7 36.4 %copy-start.12 = (bf16[4,64,2,64]{3,2,1,0:T(2,128)(2,1)}, bf16[4,64,2,64]{3,2,1,0:T(2,128)(2,1)S(1)}, u32[]{:S(2)}) copy-start(bf16[4,64,2,64]{3,2,1,0:T(2,128)(2,1)S(1)} %reshape_squeeze.9) | copy-start | bytes 196612
  106.0 1.7 copy-start.37
  106.0 64.8 %copy-start.38 = (f32[4,2,64]{2,1,0:T(2,128)}, f32[4,2,64]{2,1,0:T(2,128)S(1)}, u32[]{:S(2)}) copy-start(f32[4,2,64]{2,1,0:T(2,128)S(1)} %get-tuple-element.55) | copy-start | bytes 6148
  106.4 35.8 %copy-start.13 = (bf16[4,2,64,64]{3,2,1,0:T(8,128)(2,1)}, bf16[4,2,64,64]{3,2,1,0:T(8,128)(2,1)S(1)}, u32[]{:S(2)}) copy-start(bf16[4,2,64,64]{3,2,1,0:T(8,128)(2,1)S(1)} %convolution_convert_fusion.4) | copy-start | bytes 196612
  107.7 110.4 %reduce-scatter.13.cloned.1.call-start = ((), (), s32[]{:S(2)}) async-start(), calls=%async_computation.12 | async-start | bytes 1179648 | tf_op jit(solution)/shard_map/reduce_scatter | solution.py:19
  107.8 69.0 %copy-start.30 = (f32[1024]{0:T(1024)}, f32[1024]{0:T(1024)S(1)}, u32[]{:S(2)}) copy-start(f32[1024]{0:T(1024)S(1)} %convert_element_type.126) | copy-start | bytes 12292
  170.8 6.0 copy-start.25
  170.8 6.0 copy-start.33
  170.8 6.1 copy-start.36
  170.8 6.1 copy-start.26
  170.8 114.1 %copy-start.1 = (bf16[2,128,1024]{2,1,0:T(8,128)(2,1)S(1)}, bf16[2,128,1024]{2,1,0:T(8,128)(2,1)}, u32[]{:S(2)}) copy-start(bf16[2,128,1024]{2,1,0:T(8,128)(2,1)} %param.16) | copy-start | bytes 1572868
  172.7 2.7 copy-start.39
  175.4 82.1 %copy-start.7 = (bf16[4,64,512]{2,1,0:T(8,128)(2,1)}, bf16[4,64,512]{2,1,0:T(8,128)(2,1)S(1)}, u32[]{:S(2)}) copy-start(bf16[4,64,512]{2,1,0:T(8,128)(2,1)S(1)} %get-tuple-element.57) | copy-start | bytes 786436
  237.7 19.8 %all-to-all-start.1 = ((bf16[32,4,2,128]{3,2,1,0:T(2,128)(2,1)}), bf16[32,4,2,128]{3,2,1,0:T(2,128)(2,1)S(1)}, u32[]{:S(2)}, u32[]{:S(2)}) async-start(bf16[32,4,2,128]{3,2,1,0:T(2,128)(2,1)} %constant_dynamic-update-slice_fusion), calls=%async_computation.4 | async-start | bytes 131072 | tf_op jit(solution)/shard_map/all_to_all | solution.py:28
  247.6 132.9 %all-reduce.4.cloned.1.call-start = ((), (), s32[]{:S(2)}) async-start(), calls=%async_computation.13 | async-start | bytes 2097152 | tf_op jit(solution)/shard_map/psum | solution.py:163
  285.0 1.6 copy-start.31
  303.3 164.2 %reduce-scatter.15.cloned.1.call-start = ((), (), s32[]{:S(2)}) async-start(), calls=%async_computation.14 | async-start | bytes 1179648 | tf_op jit(solution)/shard_map/reduce_scatter | solution.py:19
  380.5 50.2 %copy-start.4 = (bf16[1024,512]{1,0:T(8,128)(2,1)S(1)}, bf16[1024,512]{1,0:T(8,128)(2,1)}, u32[]{:S(2)}) copy-start(bf16[1024,512]{1,0:T(8,128)(2,1)} %param.23) | copy-start | bytes 3145732
  380.5 51.0 %copy-start.5 = (bf16[1024,512]{1,0:T(8,128)(2,1)S(1)}, bf16[1024,512]{1,0:T(8,128)(2,1)}, u32[]{:S(2)}) copy-start(bf16[1024,512]{1,0:T(8,128)(2,1)} %param.24) | copy-start | bytes 3145732
  402.7 28.0 %copy-start.9 = (bf16[32,4,2,128]{3,2,0,1:T(2,128)(2,1)}, bf16[32,4,2,128]{3,2,0,1:T(2,128)(2,1)S(1)}, u32[]{:S(2)}) copy-start(bf16[32,4,2,128]{3,2,0,1:T(2,128)(2,1)S(1)} %copy.122) | copy-start | bytes 196612
  428.7 58.4 %copy-start.2 = (bf16[4,64,1024]{2,1,0:T(8,128)(2,1)}, bf16[4,64,1024]{2,1,0:T(8,128)(2,1)S(1)}, u32[]{:S(2)}) copy-start(bf16[4,64,1024]{2,1,0:T(8,128)(2,1)S(1)} %all_gather.21) | copy-start | bytes 1572868
  430.6 0.7 copy-start.14
  430.7 0.8 copy-start.17
  432.9 136.9 %reduce-scatter.17.cloned.1.call-start = ((), (), s32[]{:S(2)}) async-start(), calls=%async_computation.15 | async-start | bytes 1179648 | tf_op jit(solution)/shard_map/reduce_scatter | solution.py:19
  488.2 0.6 copy-start.10
  524.6 3.7 copy-start.15
  525.7 2.6 copy-start.16
  528.3 10.3 %copy-start.8 = (bf16[4,64,512]{2,1,0:T(8,128)(2,1)S(1)}, bf16[4,64,512]{2,1,0:T(8,128)(2,1)}, u32[]{:S(2)}) copy-start(bf16[4,64,512]{2,1,0:T(8,128)(2,1)} %copy-done.7) | copy-start | bytes 786436
  528.3 207.8 %reduce-scatter.19.cloned.1.call-start = ((), (), s32[]{:S(2)}) async-start(), calls=%async_computation.16 | async-start | bytes 8650752
  528.5 7.5 %copy-start.18 = (bf16[4,64,512]{2,1,0:T(8,128)(2,1)S(1)}, bf16[4,64,512]{2,1,0:T(8,128)(2,1)}, u32[]{:S(2)}) copy-start(bf16[4,64,512]{2,1,0:T(8,128)(2,1)} %copy-done.17) | copy-start | bytes 786436
  528.6 10.0 %copy-start.3 = (bf16[4,64,1024]{2,1,0:T(8,128)(2,1)S(1)}, bf16[4,64,1024]{2,1,0:T(8,128)(2,1)}, u32[]{:S(2)}) copy-start(bf16[4,64,1024]{2,1,0:T(8,128)(2,1)} %copy-done.2) | copy-start | bytes 1572868
  549.6 0.9 copy-start.19
  549.6 0.9 copy-start.28
  549.6 0.9 copy-start.32
  549.6 21.3 %copy-start.35 = (f32[128,2]{0,1:T(2,128)S(1)}, f32[128,2]{0,1:T(2,128)}, u32[]{:S(2)}) copy-start(f32[128,2]{0,1:T(2,128)} %get-tuple-element.36) | copy-start | bytes 3076
  549.6 38.7 %copy-start.11 = (bf16[4,64,128]{2,1,0:T(8,128)(2,1)S(1)}, bf16[4,64,128]{2,1,0:T(8,128)(2,1)}, u32[]{:S(2)}) copy-start(bf16[4,64,128]{2,1,0:T(8,128)(2,1)} %copy-done.10) | copy-start | bytes 196612
  549.6 38.7 %copy-start.22 = (f32[4,64]{1,0:T(4,128)S(1)}, f32[4,64]{1,0:T(4,128)}, u32[]{:S(2)}) copy-start(f32[4,64]{1,0:T(4,128)} %get-tuple-element.49) | copy-start | bytes 3076
  549.7 38.7 %copy-start.24 = (f32[4,64]{1,0:T(4,128)S(1)}, f32[4,64]{1,0:T(4,128)}, u32[]{:S(2)}) copy-start(f32[4,64]{1,0:T(4,128)} %copy-done.23) | copy-start | bytes 3076
  608.1 19.7 %all-to-all-start.3 = ((bf16[32,4,2,128]{3,2,1,0:T(2,128)(2,1)}), bf16[32,4,2,128]{3,2,1,0:T(2,128)(2,1)S(1)}, u32[]{:S(2)}, u32[]{:S(2)}) async-start(bf16[32,4,2,128]{3,2,1,0:T(2,128)(2,1)} %constant_dynamic-update-slice_fusion.32), calls=%async_computation.8 | async-start | bytes 131072 | tf_op jit(solution)/shard_map/all_to_all | solution.py:28
Sparse Core Ops, SparseCore 0:
  11.1 43.3 reduce-scatter.8
  107.8 34.2 reduce-scatter.10
  177.0 41.0 reduce-scatter.12
  303.4 77.0 all-reduce.3
  433.0 34.4 reduce-scatter.14
  528.4 41.4 reduce-scatter.16
  574.3 161.8 reduce-scatter.18
